TPU v7x, 128 devices: a whole 4x4x4 slice. The times are simulated.
128 devices in a mesh: gx: 4 (over y), gy: 4 (over z_lo, core), ta: 8 (over x, z_hi).
Axes of the slice: x: 4, y: 4, z: 4 (z_hi: 2, z_lo: 2; z = z_hi * 2 + z_lo), core: 2. Of those that a mesh axis runs over, the one named last changes fastest.
Arguments:
- tokens: bfloat16 [4, 4, 16, 128, 512], P('gx', 'gy', 'ta'), may hold values from -6 to 6
- norm_gain: float32 [512], replicated, may hold values from 0.1 to 1.9
- w_query: bfloat16 [512, 512], replicated, may hold values from -0.25 to 0.25
- w_key: bfloat16 [512, 512], replicated, may hold values from -0.25 to 0.25
- w_value: bfloat16 [512, 512], replicated, may hold values from -0.25 to 0.25
- w_proj: bfloat16 [512, 512], replicated, may hold values from -0.25 to 0.25
- temper: float32 [8], replicated, may hold values from 1 to 3
- neighbours: int32 [4, 4, 16, 27], P('gx', 'gy', 'ta'), may hold values from 0 to 255, as said below
- valid_mask: int32 [4, 4, 16, 27], P('gx', 'gy', 'ta'), may hold values from 0 to 1, as said below
- cotangent: bfloat16 [4, 4, 16, 128, 512], P('gx', 'gy', 'ta'), may hold values from -6 to 6
Outputs:
- layer_out: bfloat16 [4, 4, 16, 128, 512], P('gx', 'gy', 'ta')
- grad_tokens: float32 [4, 4, 16, 128, 512], P('gx', 'gy', 'ta')
- grad_gain: float32 [512], replicated
- grad_query: float32 [512, 512], replicated
- grad_key: float32 [512, 512], replicated
- grad_value: float32 [512, 512], replicated
- grad_proj: float32 [512, 512], replicated
- grad_temper: float32 [8], replicated
Inputs may be any that keep to these rules, and one draw needn't show every extreme that they name: `neighbours`: row (a, b, c) names the 27 blocks (i, j, k) with i - a, j - b, k - c each in -1, 0, 1 modulo 4, 4, 16, each once, in any order; block (i, j, k) is numbered (i * 4 + j) * 16 + k. `valid_mask`: the entry that names the row's own block is 1.
All inputs are finite; a program needn't handle non-finite values.
Results may differ from a plain program's by a relative error of at most 0.013.
The roundings to bfloat16 on the way count: a program that leaves them out, or rounds other values in their place, can miss the bound.
Values may be sent and summed in bfloat16 or wider, within the bound.
No kernel may reach another device: no remote copies, remote signals or barrier semaphores. Data moves between devices by JAX's collectives and lax.ppermute only.
A program may use at most 192 MiB of HBM per device.

v0:
```python
import jax
import jax.numpy as jnp
from jax import lax
from jax.sharding import PartitionSpec as P

NORM_EPS = 1e-05
HEAD_EPS = 1e-06


def extended(block, sides, width):
    for axis, dim in sides:
        count = lax.axis_size(axis)
        forward = [(i, i + 1) for i in range(count - 1)]
        forward.append((count - 1, 0))
        backward = [(target, source) for source, target in forward]
        low = lax.ppermute(
            lax.slice_in_dim(block, block.shape[dim] - width, None, axis=dim), axis, forward
        )
        high = lax.ppermute(lax.slice_in_dim(block, 0, width, axis=dim), axis, backward)
        block = jnp.concatenate([low, block, high], axis=dim)
    return block


def norm_rows(tokens):
    values = tokens.astype(jnp.float32)
    factor = lax.rsqrt(jnp.mean(values * values, axis=-1, keepdims=True) + NORM_EPS)
    return (values * factor, factor)


def norm_heads(joined, head_count):
    split_shape = joined.shape[:-1] + (head_count, joined.shape[-1] // head_count)
    shaped = joined.reshape(split_shape)
    factor = lax.rsqrt(jnp.mean(shaped * shaped, axis=-1, keepdims=True) + HEAD_EPS)
    return ((shaped * factor).reshape(joined.shape), factor)


def back_heads(normed, factor, upstream, head_count):
    split_shape = normed.shape[:-1] + (head_count, normed.shape[-1] // head_count)
    unit_rows = normed.reshape(split_shape)
    slope_rows = upstream.reshape(split_shape)
    result = factor * (
        slope_rows - unit_rows * jnp.mean(unit_rows * slope_rows, axis=-1, keepdims=True)
    )
    return result.reshape(normed.shape)


def project(inputs, weight):
    return jnp.dot(inputs, weight, preferred_element_type=jnp.float32)


def contract(left_rows, right_rows):
    return lax.dot_general(
        left_rows, right_rows, (((1,), (1,)), ((), ())), preferred_element_type=jnp.float32
    )


def outer_sum(left_rows, right_rows):
    return lax.dot_general(
        left_rows, right_rows, (((0,), (0,)), ((), ())), preferred_element_type=jnp.float32
    )


def local(
    tokens, norm_gain, w_query, w_key, w_value, w_proj, temper, neighbours, valid_mask, cotangent
):
    head_count = temper.shape[0]
    model_width = tokens.shape[-1]
    head_size = model_width // head_count
    block_rows = tokens.shape[3]
    local_t = tokens.shape[2]
    slot_count = neighbours.shape[-1]
    padded_t = local_t + 2
    score_scale = head_size ** (-0.5)
    span_x = lax.axis_size("gx")
    span_y = lax.axis_size("gy")
    span_t = local_t * lax.axis_size("ta")
    anchor_x = lax.axis_index("gx")
    anchor_y = lax.axis_index("gy")
    anchor_t = lax.axis_index("ta") * local_t
    head_ids = jnp.arange(head_count, dtype=jnp.int32)
    local_ids = jnp.arange(local_t, dtype=jnp.int32)
    unit_in, factor = norm_rows(tokens)
    hidden = (unit_in * norm_gain).astype(jnp.bfloat16)
    query_f, query_factor = norm_heads(project(hidden, w_query), head_count)
    key_f, key_factor = norm_heads(project(hidden, w_key), head_count)
    query_n = query_f.astype(jnp.bfloat16)
    key_n = key_f.astype(jnp.bfloat16)
    value_n = project(hidden, w_value).astype(jnp.bfloat16)
    back_mixed = project(cotangent, w_proj.T).astype(jnp.bfloat16)
    margin = extended(
        jnp.concatenate([key_n, value_n], axis=-1), (("gx", 0), ("gy", 1), ("ta", 2)), 1
    )
    key_pad = margin[..., :model_width]
    value_pad = margin[..., model_width:]
    key_flat = key_pad.reshape(9 * padded_t, block_rows, model_width)
    value_flat = value_pad.reshape(9 * padded_t, block_rows, model_width)

    def query_block(packed):
        query_blk, back_blk, block_ids, keep_row, local_pos = packed
        along_t = block_ids % span_t
        along_y = block_ids // span_t % span_y
        along_x = block_ids // (span_t * span_y)
        step_x = (along_x - anchor_x + 1) % span_x
        step_y = (along_y - anchor_y + 1) % span_y
        step_t = (along_t - anchor_t - local_pos + 1) % span_t + local_pos
        slot_rows = (step_x * 3 + step_y) * padded_t + step_t
        keys_all = key_flat[slot_rows].reshape(slot_count * block_rows, model_width)
        values_all = value_flat[slot_rows].reshape(slot_count * block_rows, model_width)
        key_keep = jnp.repeat(keep_row.astype(jnp.float32), block_rows)

        def query_one_head(head_id):
            query_h = lax.dynamic_slice_in_dim(query_blk, head_id * head_size, head_size, 1)
            back_h = lax.dynamic_slice_in_dim(back_blk, head_id * head_size, head_size, 1)
            key_h = lax.dynamic_slice_in_dim(keys_all, head_id * head_size, head_size, 1)
            value_h = lax.dynamic_slice_in_dim(values_all, head_id * head_size, head_size, 1)
            temp_h = temper[head_id]
            scores = contract(query_h, key_h) * score_scale
            weights = jnp.exp(temp_h * scores) * key_keep
            totals = jnp.sum(weights, axis=1)
            probs = weights / totals[:, None]
            probs_b = probs.astype(jnp.bfloat16)
            mixed_h = jnp.dot(probs_b, value_h, preferred_element_type=jnp.float32)
            slopes = contract(back_h, value_h)
            inners = jnp.sum(probs * slopes, axis=1)
            score_grad = probs * (slopes - inners[:, None])
            temper_part = jnp.sum(score_grad * scores)
            scaled = (score_grad * (temp_h * score_scale)).astype(jnp.bfloat16)
            query_grad = jnp.dot(scaled, key_h, preferred_element_type=jnp.float32)
            return (mixed_h, query_grad, totals, inners, temper_part)

        results = lax.map(query_one_head, head_ids)
        mixed_h, query_grad, totals, inners, temper_part = results[:5]
        mixed_blk = (
            jnp.transpose(mixed_h, (1, 0, 2)).reshape(block_rows, model_width).astype(jnp.bfloat16)
        )
        grad_blk = jnp.transpose(query_grad, (1, 0, 2)).reshape(block_rows, model_width)
        outs = (mixed_blk, grad_blk, jnp.stack([totals, inners]), temper_part)
        return (outs, None, None)

    scan_inputs = (query_n[0, 0], back_mixed[0, 0], neighbours[0, 0], valid_mask[0, 0], local_ids)
    mixed_all, query_grads, moments, temper_parts = lax.map(
        lambda packed: query_block(packed)[0], scan_inputs
    )
    joined = extended(
        jnp.concatenate([query_n, back_mixed], axis=-1), (("gx", 0), ("gy", 1), ("ta", 2)), 1
    )
    query_pad = joined[..., :model_width]
    back_pad = joined[..., model_width:]
    stats_pad = extended(
        moments.reshape((1, 1) + moments.shape), (("gx", 0), ("gy", 1), ("ta", 2)), 1
    )
    lists_pad = extended(
        jnp.concatenate([neighbours, valid_mask], axis=-1), (("gx", 0), ("gy", 1), ("ta", 2)), 1
    )
    query_flat = query_pad.reshape(9 * padded_t, block_rows, model_width)
    back_flat = back_pad.reshape(9 * padded_t, block_rows, model_width)
    stats_flat = stats_pad.reshape((9 * padded_t,) + moments.shape[1:])
    lists_flat = lists_pad.reshape(9 * padded_t, 2 * slot_count)
    window = (
        jnp.arange(9, dtype=jnp.int32)[:, None] * padded_t + jnp.arange(3, dtype=jnp.int32)[None, :]
    ).reshape(-1)

    def key_block(packed):
        key_blk, value_blk, local_pos = packed
        slot_rows = window + local_pos
        own_number = (anchor_x * span_y + anchor_y) * span_t + anchor_t + local_pos
        listed = lists_flat[slot_rows]
        attends = jnp.sum(
            jnp.where(listed[:, :slot_count] == own_number, listed[:, slot_count:], 0), axis=1
        )
        query_keep = jnp.repeat(attends.astype(jnp.float32), block_rows)
        queries_all = query_flat[slot_rows].reshape(-1, model_width)
        backs_all = back_flat[slot_rows].reshape(-1, model_width)
        picked = stats_flat[slot_rows]
        totals_all = jnp.transpose(picked[:, 0], (1, 0, 2)).reshape(head_count, -1)
        inners_all = jnp.transpose(picked[:, 1], (1, 0, 2)).reshape(head_count, -1)

        def key_one_head(head_id):
            query_h = lax.dynamic_slice_in_dim(queries_all, head_id * head_size, head_size, 1)
            back_h = lax.dynamic_slice_in_dim(backs_all, head_id * head_size, head_size, 1)
            key_h = lax.dynamic_slice_in_dim(key_blk, head_id * head_size, head_size, 1)
            value_h = lax.dynamic_slice_in_dim(value_blk, head_id * head_size, head_size, 1)
            temp_h = temper[head_id]
            scores = contract(query_h, key_h) * score_scale
            probs = jnp.exp(temp_h * scores) * query_keep[:, None] / totals_all[head_id][:, None]
            probs_b = probs.astype(jnp.bfloat16)
            slopes = contract(back_h, value_h)
            score_grad = probs * (slopes - inners_all[head_id][:, None])
            scaled = (score_grad * (temp_h * score_scale)).astype(jnp.bfloat16)
            key_grad = outer_sum(scaled, query_h)
            value_grad = outer_sum(probs_b, back_h)
            return (key_grad, value_grad)

        key_grad, value_grad = lax.map(key_one_head, head_ids)
        key_out = jnp.transpose(key_grad, (1, 0, 2)).reshape(block_rows, model_width)
        value_out = jnp.transpose(value_grad, (1, 0, 2)).reshape(block_rows, model_width)
        return (key_out, value_out)

    key_grads, value_grads = lax.map(key_block, (key_n[0, 0], value_n[0, 0], local_ids))
    layer_out = project(mixed_all, w_proj).astype(jnp.bfloat16).reshape(tokens.shape)
    query_d = back_heads(
        query_f, query_factor, query_grads.reshape(tokens.shape), head_count
    ).astype(jnp.bfloat16)
    key_d = back_heads(key_f, key_factor, key_grads.reshape(tokens.shape), head_count).astype(
        jnp.bfloat16
    )
    value_d = value_grads.reshape(tokens.shape).astype(jnp.bfloat16)
    hidden_rows = hidden.reshape(-1, model_width)
    back_hidden = (
        project(query_d, w_query.T) + project(key_d, w_key.T) + project(value_d, w_value.T)
    )
    slope_in = back_hidden * norm_gain
    grad_tokens = factor * (
        slope_in - unit_in * jnp.mean(slope_in * unit_in, axis=-1, keepdims=True)
    )
    gain_part = jnp.sum((back_hidden * unit_in).reshape(-1, model_width), axis=0)
    grad_query, grad_key, grad_value, grad_proj, grad_gain, grad_temper = lax.psum(
        (
            outer_sum(hidden_rows, query_d.reshape(-1, model_width)),
            outer_sum(hidden_rows, key_d.reshape(-1, model_width)),
            outer_sum(hidden_rows, value_d.reshape(-1, model_width)),
            outer_sum(mixed_all.reshape(-1, model_width), cotangent.reshape(-1, model_width)),
            gain_part,
            jnp.sum(temper_parts, axis=0),
        ),
        ("gx", "gy", "ta"),
    )
    return (
        layer_out,
        grad_tokens,
        grad_gain,
        grad_query,
        grad_key,
        grad_value,
        grad_proj,
        grad_temper,
    )


def solution(mesh):
    placed = (
        P("gx", "gy", "ta", None, None),
        P(),
        P(),
        P(),
        P(),
        P(),
        P(),
        P("gx", "gy", "ta", None),
        P("gx", "gy", "ta", None),
        P("gx", "gy", "ta", None, None),
    )
    return jax.shard_map(
        local,
        mesh=mesh,
        in_specs=placed,
        out_specs=(
            P("gx", "gy", "ta", None, None),
            P("gx", "gy", "ta", None, None),
            P(),
            P(),
            P(),
            P(),
            P(),
            P(),
        ),
        check_vma=False,
    )
```

profile of v0, /device:TPU:1, one launch (start us, length us, event | category | flops | bytes accessed | tf_op | source)
XLA Modules:
  0.0 1014.8 jit_solution(3526147688756526316)
XLA Ops:
  17.5 11.1 %collective-permute-done = bf16[1,1,2,128,1024]{4,3,2,1,0:T(8,128)(2,1)S(1)} collective-permute-done((bf16[1,1,2,128,1024]{4,3,2,1,0:T(8,128)(2,1)}, bf16[1,1,2,128,1024]{4,3,2,1,0:T(8,128)(2,1)S(1)}, u32[]{:S(2)}, u32[]{:S(2)}) %collective-permute-start) | collective-permute-done | bytes 524320 | tf_op jit(solution)/shard_map/ppermute | solution.py:16
  42.1 11.8 %collective-permute-done.6 = bf16[1,1,2,128,1024]{4,3,2,1,0:T(8,128)(2,1)S(1)} collective-permute-done((bf16[1,1,2,128,1024]{4,3,2,1,0:T(8,128)(2,1)S(1)}, bf16[1,1,2,128,1024]{4,3,2,1,0:T(8,128)(2,1)S(1)}, u32[]{:S(2)}, u32[]{:S(2)}) %collective-permute-start.6) | collective-permute-done | bytes 524320 | tf_op jit(solution)/shard_map/ppermute | solution.py:16
  56.5 10.6 %collective-permute-done.2 = bf16[3,1,2,128,1024]{4,3,2,1,0:T(8,128)(2,1)} collective-permute-done((bf16[3,1,2,128,1024]{4,3,2,1,0:T(8,128)(2,1)}, bf16[3,1,2,128,1024]{4,3,2,1,0:T(8,128)(2,1)}, u32[]{:S(2)}, u32[]{:S(2)}) %collective-permute-start.2) | collective-permute-done | bytes 1572896 | tf_op jit(solution)/shard_map/ppermute | solution.py:16
  67.1 3.2 collective-permute-done.3
  70.3 3.4 pad_maximum_fusion.2
  76.4 3.3 collective-permute-start.4
  90.1 111.9 %collective-permute-done.14 = s32[3,1,2,54]{3,2,1,0:T(2,128)S(1)} collective-permute-done((s32[3,1,2,54]{3,2,1,0:T(2,128)S(1)}, s32[3,1,2,54]{3,2,1,0:T(2,128)S(1)}, u32[]{:S(2)}, u32[]{:S(2)}) %collective-permute-start.14) | collective-permute-done | bytes 1328 | tf_op jit(solution)/shard_map/ppermute | solution.py:16
  201.9 4.1 collective-permute-done.15
  217.0 3.4 pad_maximum_fusion.3
  224.4 3.7 collective-permute-start.11
  228.2 8.6 pad_maximum_fusion
  236.8 8.6 fusion.110
  246.2 289.6 %while.106 = (s32[]{:T(128)}, bf16[2,128,512]{1,2,0:T(8,128)(2,1)}, f32[2,128,512]{1,2,0:T(8,128)}, f32[2,2,8,128]{3,2,1,0:T(8,128)S(1)}, f32[2,8]{1,0:T(2,128)S...) while((s32[]{:T(128)}, bf16[2,128,512]{1,2,0:T(8,128)(2,1)}, ...), condition=%wide.region_9.10_spmd.clone, body=%wide.region_3.9_spmd.clone.sunk | while | flops 238441568 | bytes 40497868 | solution.py:141
  247.5 5.0 gather_fusion.4
  252.5 4.9 gather_fusion.5
  257.5 132.1 %while.109 = (s32[]{:T(128)}, bf16[8,128,64]{1,2,0:T(8,128)(2,1)S(1)}, f32[8,128,64]{1,2,0:T(8,128)S(1)}, f32[8,128]{1,0:T(8,128)S(1)}, f32[8,128]{1,0:T(8,128)S...) while((s32[]{:T(128)}, ...), condition=%wide.region_8.8_spmd.clone, body=%wide.region_4.7_spmd.clone.sunk | while | flops 238436096 | bytes 25008588 | solution.py:131
  392.3 5.0 gather_fusion.4
  397.3 4.9 gather_fusion.5
  402.3 132.1 %while.109 = (s32[]{:T(128)}, bf16[8,128,64]{1,2,0:T(8,128)(2,1)S(1)}, f32[8,128,64]{1,2,0:T(8,128)S(1)}, f32[8,128]{1,0:T(8,128)S(1)}, f32[8,128]{1,0:T(8,128)S...) while((s32[]{:T(128)}, ...), condition=%wide.region_8.8_spmd.clone, body=%wide.region_4.7_spmd.clone.sunk | while | flops 238436096 | bytes 25008588 | solution.py:131
  538.6 7.7 pad_maximum_fusion.1
  546.3 8.5 fusion.109
  558.0 3.1 collective-permute-start.20
  564.7 5.1 collective-permute-start.23
  573.1 263.4 %while.108 = (s32[]{:T(128)}, f32[2,128,512]{1,2,0:T(8,128)}, bf16[2,128,512]{1,2,0:T(8,128)(2,1)}, s32[2]{0:T(128)S(1)}, bf16[36,128,512]{2,1,0:T(8,128)(2,1)},...) while((s32[]{:T(128)}, f32[2,128,512]{1,2,0:T(8,128)}, ...), condition=%wide.region_15.16_spmd.clone, body=%wide.region_11.15_spmd.clone.sunk | while | flops 230034704 | bytes 25472284 | solution.py:199
  577.5 5.0 gather_fusion
  582.6 4.9 gather_fusion.2
  588.2 113.4 %while.110 = (s32[]{:T(128)}, f32[8,128,64]{1,2,0:T(8,128)}, bf16[8,128,64]{1,2,0:T(8,128)(2,1)}, s32[8]{0:T(128)S(1)}, bf16[3456,512]{1,0:T(8,128)(2,1)}, /*ind...) while((s32[]{:T(128)}, f32[8,128,64]{1,2,0:T(8,128)}, ...), condition=%wide.region_14.14_spmd.clone, body=%wide.region_13.13_spmd.clone.sunk | while | flops 230031360 | bytes 9096589 | solution.py:194
  592.8 3.3 fusion.158
  596.1 3.6 fusion.159
  606.9 3.3 fusion.158
  610.3 3.6 fusion.159
  621.1 3.3 fusion.158
  624.4 3.6 fusion.159
  635.3 3.3 fusion.158
  638.6 3.6 fusion.159
  649.5 3.3 fusion.158
  652.8 3.6 fusion.159
  663.7 3.3 fusion.158
  667.0 3.6 fusion.159
  677.8 3.3 fusion.158
  681.2 3.6 fusion.159
  692.0 3.3 fusion.158
  695.3 3.6 fusion.159
  709.2 5.0 gather_fusion
  714.3 4.9 gather_fusion.2
  719.9 113.4 %while.110 = (s32[]{:T(128)}, f32[8,128,64]{1,2,0:T(8,128)}, bf16[8,128,64]{1,2,0:T(8,128)(2,1)}, s32[8]{0:T(128)S(1)}, bf16[3456,512]{1,0:T(8,128)(2,1)}, /*ind...) while((s32[]{:T(128)}, f32[8,128,64]{1,2,0:T(8,128)}, ...), condition=%wide.region_14.14_spmd.clone, body=%wide.region_13.13_spmd.clone.sunk | while | flops 230031360 | bytes 9096589 | solution.py:194
  724.4 3.3 fusion.158
  727.8 3.6 fusion.159
  738.6 3.3 fusion.158
  741.9 3.6 fusion.159
  752.8 3.3 fusion.158
  756.1 3.6 fusion.159
  767.0 3.3 fusion.158
  770.3 3.6 fusion.159
  781.2 3.3 fusion.158
  784.5 3.6 fusion.159
  795.4 3.3 fusion.158
  798.7 3.6 fusion.159
  809.5 3.3 fusion.158
  812.8 3.6 fusion.159
  823.7 3.3 fusion.158
  827.0 3.6 fusion.159
  848.6 66.4 %all-reduce = (f32[512]{0:T(512)}, f32[8]{0:T(128)}) all-reduce(f32[512]{0:T(512)S(1)} %get-tuple-element.752, f32[8]{0:T(128)S(1)} %reduce_sum.117), channel_id=1, replica_groups=mesh['gx'=4,'gy'=4,'ta'=8] {'gx','gy','ta'}, use_global_device_ids=true, to_apply=%region_19.20 | all-reduce | flops 520 | bytes 4160 | tf_op jit(solution)/shard_map/psum | solution.py:217
  916.0 85.3 %all-reduce.4.cloned.1.call-done = (f32[512,512]{1,0:T(8,128)}, f32[512,512]{1,0:T(8,128)}, f32[512,512]{1,0:T(8,128)}, f32[512,512]{1,0:T(8,128)}) async-done(((f32[512,512]{1,0:T(8,128)}, f32[512,512]{1,0:T(8,128)}, f32[512,512]{1,0:T(8,128)}, f32[512,512]{1,0:T(8,128)}), (f32[512,512]{1,0:T(8,128)}, f32[512,512]{1,0:T(8,128)}, f32[512,512]{1,0:T(8,128)}, ...) | async-done | bytes 4194320 | tf_op jit(solution)/shard_map/psum | solution.py:217
  (547 shorter events, 384.2 us)
Async XLA Ops:
  7.2 4.9 copy-start
  7.2 4.9 copy-start.3
  7.2 4.9 copy-start.32
  7.2 994.1 %all-reduce.4.cloned.1.call-start = ((), (), s32[]{:S(2)}) async-start(), calls=%async_computation | async-start | bytes 8388608 | tf_op jit(solution)/shard_map/psum | solution.py:217
  8.4 8.5 copy-start.38
  9.9 7.0 copy-start.26
  10.2 2.3 copy-start.34
  12.1 216.1 %copy-start.5 = (bf16[2,128,512]{2,1,0:T(8,128)(2,1)}, bf16[2,128,512]{2,1,0:T(8,128)(2,1)S(1)}, u32[]{:S(2)}) copy-start(bf16[2,128,512]{2,1,0:T(8,128)(2,1)S(1)} %get-tuple-element.1504) | copy-start | bytes 786436
  12.4 215.7 %copy-start.7 = (bf16[2,128,512]{2,1,0:T(8,128)(2,1)}, bf16[2,128,512]{2,1,0:T(8,128)(2,1)S(1)}, u32[]{:S(2)}) copy-start(bf16[2,128,512]{2,1,0:T(8,128)(2,1)S(1)} %convolution_convert_fusion.1) | copy-start | bytes 786436
  13.3 15.3 %collective-permute-start = (bf16[1,1,2,128,1024]{4,3,2,1,0:T(8,128)(2,1)}, bf16[1,1,2,128,1024]{4,3,2,1,0:T(8,128)(2,1)S(1)}, u32[]{:S(2)}, u32[]{:S(2)}) collective-permute-start(bf16[1,1,2,128,1024]{4,3,2,1,0:T(8,128)(2,1)} %pad_maximum_fusion.6), channel_id=1, source_target_pairs={{0,32},{32,64},{64,96},{96,0},{1,33},{33,65},{65,97},{97,1},{2,34}... | collective-permute-start | bytes 1572872 | tf_op jit(solution)/shard_map/ppermute | solution.py:16
  15.5 13.1 %collective-permute-start.1 = (bf16[1,1,2,128,1024]{4,3,2,1,0:T(8,128)(2,1)}, bf16[1,1,2,128,1024]{4,3,2,1,0:T(8,128)(2,1)S(1)}, u32[]{:S(2)}, u32[]{:S(2)}) collective-permute-start(bf16[1,1,2,128,1024]{4,3,2,1,0:T(8,128)(2,1)} %pad_maximum_fusion.6), channel_id=1, source_target_pairs={{32,0},{64,32},{96,64},{0,96},{33,1},{65,33},{97,65},{1,97},{34,2}... | collective-permute-start | bytes 1572872 | tf_op jit(solution)/shard_map/ppermute | solution.py:19
  17.5 16.4 %copy-start.17 = (f32[2,128,512]{1,2,0:T(8,128)}, f32[2,128,512]{1,2,0:T(8,128)S(1)}, u32[]{:S(2)}) copy-start(f32[2,128,512]{1,2,0:T(8,128)S(1)} %copy.28) | copy-start | bytes 1572868
  28.6 10.6 %copy-start.11 = (bf16[1,1,2,128,1024]{4,3,2,1,0:T(8,128)(2,1)}, bf16[1,1,2,128,1024]{4,3,2,1,0:T(8,128)(2,1)S(1)}, u32[]{:S(2)}) copy-start(bf16[1,1,2,128,1024]{4,3,2,1,0:T(8,128)(2,1)S(1)} %collective-permute-done.1) | copy-start | bytes 1572868
  30.0 37.1 %collective-permute-start.2 = (bf16[3,1,2,128,1024]{4,3,2,1,0:T(8,128)(2,1)}, bf16[3,1,2,128,1024]{4,3,2,1,0:T(8,128)(2,1)}, u32[]{:S(2)}, u32[]{:S(2)}) collective-permute-start(bf16[3,1,2,128,1024]{4,3,2,1,0:T(8,128)(2,1)} %pad_maximum_fusion.4), channel_id=1, source_target_pairs={{0,8},{8,16},{16,24},{24,0},{1,9},{9,17},{17,25},{25,1},{2,10},{10... | collective-permute-start | bytes 4718600 | tf_op jit(solution)/shard_map/ppermute | solution.py:16
  32.9 37.4 %collective-permute-start.3 = (bf16[3,1,2,128,1024]{4,3,2,1,0:T(8,128)(2,1)}, bf16[3,1,2,128,1024]{4,3,2,1,0:T(8,128)(2,1)}, u32[]{:S(2)}, u32[]{:S(2)}) collective-permute-start(bf16[3,1,2,128,1024]{4,3,2,1,0:T(8,128)(2,1)} %pad_maximum_fusion.4), channel_id=1, source_target_pairs={{8,0},{16,8},{24,16},{0,24},{9,1},{17,9},{25,17},{1,25},{10,2},{18... | collective-permute-start | bytes 4718600 | tf_op jit(solution)/shard_map/ppermute | solution.py:19
  39.2 31.0 %copy-start.12 = (bf16[1,1,2,128,1024]{4,3,2,1,0:T(8,128)(2,1)S(1)}, bf16[1,1,2,128,1024]{4,3,2,1,0:T(8,128)(2,1)}, u32[]{:S(2)}) copy-start(bf16[1,1,2,128,1024]{4,3,2,1,0:T(8,128)(2,1)} %copy-done.11) | copy-start | bytes 1572868
  39.3 14.6 %collective-permute-start.6 = (bf16[1,1,2,128,1024]{4,3,2,1,0:T(8,128)(2,1)S(1)}, bf16[1,1,2,128,1024]{4,3,2,1,0:T(8,128)(2,1)S(1)}, u32[]{:S(2)}, u32[]{:S(2)}) collective-permute-start(bf16[1,1,2,128,1024]{4,3,2,1,0:T(8,128)(2,1)S(1)} %pad_maximum_fusion.7), channel_id=1, source_target_pairs={{0,32},{32,64},{64,96},{96,0},{1,33},{33,65},{65,97},{97,1},{2,34}... | collective-permute-start | bytes 1572872 | tf_op jit(solution)/shard_map/ppermute | solution.py:16
  40.7 13.2 %collective-permute-start.7 = (bf16[1,1,2,128,1024]{4,3,2,1,0:T(8,128)(2,1)S(1)}, bf16[1,1,2,128,1024]{4,3,2,1,0:T(8,128)(2,1)S(1)}, u32[]{:S(2)}, u32[]{:S(2)}) collective-permute-start(bf16[1,1,2,128,1024]{4,3,2,1,0:T(8,128)(2,1)S(1)} %pad_maximum_fusion.7), channel_id=1, source_target_pairs={{32,0},{64,32},{96,64},{0,96},{33,1},{65,33},{97,65},{1,97},{34,2}... | collective-permute-start | bytes 1572872 | tf_op jit(solution)/shard_map/ppermute | solution.py:19
  53.9 163.1 %copy-start.9 = (bf16[1,1,2,128,1024]{4,3,2,1,0:T(8,128)(2,1)}, bf16[1,1,2,128,1024]{4,3,2,1,0:T(8,128)(2,1)S(1)}, u32[]{:S(2)}) copy-start(bf16[1,1,2,128,1024]{4,3,2,1,0:T(8,128)(2,1)S(1)} %collective-permute-done.6) | copy-start | bytes 1572868
  53.9 163.1 %copy-start.10 = (bf16[1,1,2,128,1024]{4,3,2,1,0:T(8,128)(2,1)}, bf16[1,1,2,128,1024]{4,3,2,1,0:T(8,128)(2,1)S(1)}, u32[]{:S(2)}) copy-start(bf16[1,1,2,128,1024]{4,3,2,1,0:T(8,128)(2,1)S(1)} %collective-permute-done.7) | copy-start | bytes 1572868
  55.4 161.5 %collective-permute-start.8 = (bf16[3,1,2,128,1024]{4,3,2,1,0:T(8,128)(2,1)}, bf16[3,1,2,128,1024]{4,3,2,1,0:T(8,128)(2,1)}, u32[]{:S(2)}, u32[]{:S(2)}) collective-permute-start(bf16[3,1,2,128,1024]{4,3,2,1,0:T(8,128)(2,1)} %pad_maximum_fusion.5), channel_id=1, source_target_pairs={{0,8},{8,16},{16,24},{24,0},{1,9},{9,17},{17,25},{25,1},{2,10},{10... | collective-permute-start | bytes 4718600 | tf_op jit(solution)/shard_map/ppermute | solution.py:16
  56.5 160.5 %collective-permute-start.9 = (bf16[3,1,2,128,1024]{4,3,2,1,0:T(8,128)(2,1)}, bf16[3,1,2,128,1024]{4,3,2,1,0:T(8,128)(2,1)}, u32[]{:S(2)}, u32[]{:S(2)}) collective-permute-start(bf16[3,1,2,128,1024]{4,3,2,1,0:T(8,128)(2,1)} %pad_maximum_fusion.5), channel_id=1, source_target_pairs={{8,0},{16,8},{24,16},{0,24},{9,1},{17,9},{25,17},{1,25},{10,2},{18... | collective-permute-start | bytes 4718600 | tf_op jit(solution)/shard_map/ppermute | solution.py:19
  73.7 8.2 copy-start.40
  73.7 8.2 copy-start.41
  76.4 151.8 %collective-permute-start.4 = (bf16[3,3,1,128,1024]{4,3,2,1,0:T(8,128)(2,1)}, bf16[3,3,1,128,1024]{4,3,2,1,0:T(8,128)(2,1)}, u32[]{:S(2)}, u32[]{:S(2)}) collective-permute-start(bf16[3,3,1,128,1024]{4,3,2,1,0:T(8,128)(2,1)} %get-tuple-element.890), channel_id=1, source_target_pairs={{0,1},{1,2},{2,3},{3,4},{4,5},{5,6},{6,7},{7,0},{8,9},{9,10},{10,1... | collective-permute-start | bytes 7077896 | tf_op jit(solution)/shard_map/ppermute | solution.py:16
  79.7 148.5 %collective-permute-start.5 = (bf16[3,3,1,128,1024]{4,3,2,1,0:T(8,128)(2,1)}, bf16[3,3,1,128,1024]{4,3,2,1,0:T(8,128)(2,1)}, u32[]{:S(2)}, u32[]{:S(2)}) collective-permute-start(bf16[3,3,1,128,1024]{4,3,2,1,0:T(8,128)(2,1)} %get-tuple-element.891), channel_id=1, source_target_pairs={{1,0},{2,1},{3,2},{4,3},{5,4},{6,5},{7,6},{0,7},{9,8},{10,9},{11,1... | collective-permute-start | bytes 7077896 | tf_op jit(solution)/shard_map/ppermute | solution.py:19
  81.9 4.0 collective-permute-start.12
  86.0 2.8 collective-permute-start.13
  88.9 113.1 %collective-permute-start.14 = (s32[3,1,2,54]{3,2,1,0:T(2,128)S(1)}, s32[3,1,2,54]{3,2,1,0:T(2,128)S(1)}, u32[]{:S(2)}, u32[]{:S(2)}) collective-permute-start(s32[3,1,2,54]{3,2,1,0:T(2,128)S(1)} %pad_add_fusion.2), channel_id=1, source_target_pairs={{0,8},{8,16},{16,24},{24,0},{1,9},{9,17},{17,25},{25,1},{2,10},{10... | collective-permute-start | bytes 3896 | tf_op jit(solution)/shard_map/ppermute | solution.py:16
  201.9 4.1 collective-permute-start.15
  206.1 6.1 collective-permute-start.16
  212.3 4.0 collective-permute-start.17
  220.4 7.7 copy-start.13
  223.0 315.6 %collective-permute-start.10 = (bf16[3,3,1,128,1024]{4,3,2,1,0:T(8,128)(2,1)}, bf16[3,3,1,128,1024]{4,3,2,1,0:T(8,128)(2,1)}, u32[]{:S(2)}, u32[]{:S(2)}) collective-permute-start(bf16[3,3,1,128,1024]{4,3,2,1,0:T(8,128)(2,1)} %get-tuple-element.888), channel_id=1, source_target_pairs={{0,1},{1,2},{2,3},{3,4},{4,5},{5,6},{6,7},{7,0},{8,9},{9,10},{10,1... | collective-permute-start | bytes 7077896 | tf_op jit(solution)/shard_map/ppermute | solution.py:16
  224.4 314.2 %collective-permute-start.11 = (bf16[3,3,1,128,1024]{4,3,2,1,0:T(8,128)(2,1)}, bf16[3,3,1,128,1024]{4,3,2,1,0:T(8,128)(2,1)}, u32[]{:S(2)}, u32[]{:S(2)}) collective-permute-start(bf16[3,3,1,128,1024]{4,3,2,1,0:T(8,128)(2,1)} %get-tuple-element.889), channel_id=1, source_target_pairs={{1,0},{2,1},{3,2},{4,3},{5,4},{6,5},{7,6},{0,7},{9,8},{10,9},{11,1... | collective-permute-start | bytes 7077896 | tf_op jit(solution)/shard_map/ppermute | solution.py:19
  236.8 9.4 copy-start.43
  535.8 22.1 %collective-permute-start.18 = (f32[1,1,2,2,8,128]{5,4,3,2,1,0:T(8,128)S(1)}, f32[1,1,2,2,8,128]{5,4,3,2,1,0:T(8,128)S(1)}, u32[]{:S(2)}, u32[]{:S(2)}) collective-permute-start(f32[1,1,2,2,8,128]{5,4,3,2,1,0:T(8,128)S(1)} %bitcast.281), channel_id=1, source_target_pairs={{0,32},{32,64},{64,96},{96,0},{1,33},{33,65},{65,97},{97,1},{2,34}... | collective-permute-start | bytes 49160 | tf_op jit(solution)/shard_map/ppermute | solution.py:16
  537.2 20.7 %collective-permute-start.19 = (f32[1,1,2,2,8,128]{5,4,3,2,1,0:T(8,128)S(1)}, f32[1,1,2,2,8,128]{5,4,3,2,1,0:T(8,128)S(1)}, u32[]{:S(2)}, u32[]{:S(2)}) collective-permute-start(f32[1,1,2,2,8,128]{5,4,3,2,1,0:T(8,128)S(1)} %bitcast.282), channel_id=1, source_target_pairs={{32,0},{64,32},{96,64},{0,96},{33,1},{65,33},{97,65},{1,97},{34,2}... | collective-permute-start | bytes 49160 | tf_op jit(solution)/shard_map/ppermute | solution.py:19
  546.3 8.6 copy-start.20
  546.3 9.6 copy-start.18
  546.3 9.6 copy-start.37
  554.9 2.9 copy-start.30
  556.0 13.8 %copy-start.4 = (bf16[1,1,2,128,512]{4,3,2,1,0:T(8,128)(2,1)S(1)}, bf16[1,1,2,128,512]{4,3,2,1,0:T(8,128)(2,1)}, u32[]{:S(2)}) copy-start(bf16[1,1,2,128,512]{4,3,2,1,0:T(8,128)(2,1)} %param.18) | copy-start | bytes 786436
  556.0 13.8 %copy-start.33 = (f32[512]{0:T(512)S(1)}, f32[512]{0:T(512)}, u32[]{:S(2)}) copy-start(f32[512]{0:T(512)} %param.19) | copy-start | bytes 6148
  556.0 13.8 %copy-start.39 = (f32[2,128]{1,0:T(2,128)S(1)}, f32[2,128]{1,0:T(2,128)}, u32[]{:S(2)}) copy-start(f32[2,128]{1,0:T(2,128)} %copy-done.38) | copy-start | bytes 3076
  556.3 16.8 %copy-start.2 = (s32[36,54]{1,0:T(8,128)S(1)}, s32[36,54]{1,0:T(8,128)}, u32[]{:S(2)}) copy-start(s32[36,54]{1,0:T(8,128)} %reshape.687) | copy-start | bytes 23332
  556.3 16.8 %copy-start.6 = (bf16[2,128,512]{2,1,0:T(8,128)(2,1)S(1)}, bf16[2,128,512]{2,1,0:T(8,128)(2,1)}, u32[]{:S(2)}) copy-start(bf16[2,128,512]{2,1,0:T(8,128)(2,1)} %copy-done.5) | copy-start | bytes 786436
  556.3 16.8 %copy-start.8 = (bf16[2,128,512]{2,1,0:T(8,128)(2,1)S(1)}, bf16[2,128,512]{2,1,0:T(8,128)(2,1)}, u32[]{:S(2)}) copy-start(bf16[2,128,512]{2,1,0:T(8,128)(2,1)} %copy-done.7) | copy-start | bytes 786436
  556.3 16.8 %copy-start.42 = (s32[9]{0:T(128)S(1)}, s32[9]{0:T(128)}, u32[]{:S(2)}) copy-start(s32[9]{0:T(128)} %iota_multiply_fusion) | copy-start | bytes 112
  557.7 15.4 %copy-start.21 = (bf16[2,128,512]{2,1,0:T(8,128)(2,1)}, bf16[2,128,512]{2,1,0:T(8,128)(2,1)S(1)}, u32[]{:S(2)}) copy-start(bf16[2,128,512]{2,1,0:T(8,128)(2,1)S(1)} %multiply_convert_fusion.3) | copy-start | bytes 786436
  558.0 5.3 collective-permute-start.20
  561.0 3.6 collective-permute-start.21
  564.6 6.9 collective-permute-start.22
  564.7 6.8 collective-permute-start.23
  573.1 265.6 %copy-start.35 = (f32[2,128,8]{1,2,0:T(8,128)S(1)}, f32[2,128,8]{1,2,0:T(8,128)}, u32[]{:S(2)}) copy-start(f32[2,128,8]{1,2,0:T(8,128)} %copy-done.34) | copy-start | bytes 24580
  836.6 4.5 copy-start.15
  836.6 4.5 copy-start.27
  838.7 5.2 copy-start.23
  842.5 2.9 copy-start.25
  842.5 2.9 copy-start.31
  843.9 2.5 copy-start.22
  845.3 2.5 copy-start.24
  1001.3 4.7 copy-start.29
  1001.3 5.7 copy-start.28
  (20 other events, 24.6 us)
Sparse Core Ops, SparseCore 0:
  845.5 155.8 all-reduce.3
where the time goes:
time: 1020 us; the launch traced here: 1010 us
  matrix products  305 us (30%)
  waiting for transfers between devices  247 us (24%)
  local copies, waits for them, and re-layouts  172 us (17%)
  loops' own time  105 us (10%)
  blocking collectives  66.4 us (7%)
  other arithmetic  62.9 us (6%)
  starting transfers between devices  41.2 us (4%)
  between operations  14.6 us (1%)
    ppermute x12, waiting for transfers between devices, extended(): lax.ppermute(lax.slice_in_dim(block, block.shape[dim] - width, None, axis...  151 us
    dot_general x48, matrix products, contract(): lax.dot_general(left_rows, right_rows, (((1,), (1,)), ((), ())), preferre...  113 us
    dot_general x36, matrix products, outer_sum(): lax.dot_general(left_rows, right_rows, (((0,), (0,)), ((), ())), preferre...  107 us
    psum x1, waiting for transfers between devices, local(): lax.psum((outer_sum(hidden_rows, query_d.reshape(-1, model_width)), outer...  85.3 us
    psum x1, blocking collectives, local(): lax.psum((outer_sum(hidden_rows, query_d.reshape(-1, model_width)), outer...  66.4 us
    another operation x2, loops' own time, key_block(): key_grad, value_grad = lax.map(key_one_head, head_ids)  52.2 us
    another operation x2, loops' own time, query_block(): results = lax.map(query_one_head, head_ids)  51.3 us
    dot_general x16, matrix products, query_one_head(): query_grad = jnp.dot(scaled, key_h, preferred_element_type=jnp.float32)  43.6 us
  transfers between devices with their start and end apart: 25, of which 13 were waited for; matrix products, arithmetic and copies ran while one was open for 28% of the time, Pallas kernels for 0%

commit v1 on v0

--- a/solution.py
+++ b/solution.py
@@ -215,15 +215,18 @@
     )
     gain_part = jnp.sum((back_hidden * unit_in).reshape(-1, model_width), axis=0)
     grad_query, grad_key, grad_value, grad_proj, grad_gain, grad_temper = lax.psum(
-        (
-            outer_sum(hidden_rows, query_d.reshape(-1, model_width)),
-            outer_sum(hidden_rows, key_d.reshape(-1, model_width)),
-            outer_sum(hidden_rows, value_d.reshape(-1, model_width)),
-            outer_sum(mixed_all.reshape(-1, model_width), cotangent.reshape(-1, model_width)),
-            gain_part,
-            jnp.sum(temper_parts, axis=0),
+        lax.psum(
+            (
+                outer_sum(hidden_rows, query_d.reshape(-1, model_width)),
+                outer_sum(hidden_rows, key_d.reshape(-1, model_width)),
+                outer_sum(hidden_rows, value_d.reshape(-1, model_width)),
+                outer_sum(mixed_all.reshape(-1, model_width), cotangent.reshape(-1, model_width)),
+                gain_part,
+                jnp.sum(temper_parts, axis=0),
+            ),
+            ("gy", "ta"),
         ),
-        ("gx", "gy", "ta"),
+        "gx",
     )
     return (
         layer_out,

time: 1020 us -> 1070 us (1.049)
  waiting for transfers between devices: 247 us -> 288 us
  blocking collectives: 66.4 us -> 78.1 us
    psum x1, waiting for transfers between devices: 85.3 us -> 113 us  [local(): lax.psum((outer_sum(hidden_rows, query_d.reshape(-1, model_width)), outer...]
    psum x0 -> x1, waiting for transfers between devices: none -> 13.3 us  [local(): lax.psum(lax.psum((outer_sum(hidden_rows, query_d.reshape(-1, model_width...]
  transfers between devices with their start and end apart: 25 -> 26, of which waited for: 13 -> 14; matrix products, arithmetic and copies ran while one was open for 28% -> 27% of each run, Pallas kernels for 0% -> 0%
where the time goes in v1:
time: 1070 us
  matrix products  305 us (29%)
  waiting for transfers between devices  288 us (27%)
  local copies, waits for them, and re-layouts  172 us (16%)
  loops' own time  105 us (10%)
  blocking collectives  78.1 us (7%)
  other arithmetic  62.9 us (6%)
  starting transfers between devices  41.2 us (4%)
  between operations  14.6 us (1%)
    ppermute x12, waiting for transfers between devices, extended(): lax.ppermute(lax.slice_in_dim(block, block.shape[dim] - width, None, axis...  151 us
    dot_general x48, matrix products, contract(): lax.dot_general(left_rows, right_rows, (((1,), (1,)), ((), ())), preferre...  113 us
    psum x1, waiting for transfers between devices, local(): lax.psum((outer_sum(hidden_rows, query_d.reshape(-1, model_width)), outer...  113 us
    dot_general x36, matrix products, outer_sum(): lax.dot_general(left_rows, right_rows, (((0,), (0,)), ((), ())), preferre...  107 us
    psum x1, blocking collectives, local(): lax.psum((outer_sum(hidden_rows, query_d.reshape(-1, model_width)), outer...  68.2 us
    another operation x2, loops' own time, key_block(): key_grad, value_grad = lax.map(key_one_head, head_ids)  52.2 us
    another operation x2, loops' own time, query_block(): results = lax.map(query_one_head, head_ids)  51.3 us
    dot_general x16, matrix products, query_one_head(): query_grad = jnp.dot(scaled, key_h, preferred_element_type=jnp.float32)  43.6 us
  transfers between devices with their start and end apart: 26, of which 14 were waited for; matrix products, arithmetic and copies ran while one was open for 27% of the time, Pallas kernels for 0%

profile of v1, /device:TPU:1, one launch (start us, length us, event | category | flops | bytes accessed | tf_op | source)
XLA Modules:
  0.0 1067.1 jit_solution(4349499746428530813)
XLA Ops:
  17.5 11.1 %collective-permute-done = bf16[1,1,2,128,1024]{4,3,2,1,0:T(8,128)(2,1)S(1)} collective-permute-done((bf16[1,1,2,128,1024]{4,3,2,1,0:T(8,128)(2,1)}, bf16[1,1,2,128,1024]{4,3,2,1,0:T(8,128)(2,1)S(1)}, u32[]{:S(2)}, u32[]{:S(2)}) %collective-permute-start) | collective-permute-done | bytes 524320 | tf_op jit(solution)/shard_map/ppermute | solution.py:16
  42.1 11.8 %collective-permute-done.6 = bf16[1,1,2,128,1024]{4,3,2,1,0:T(8,128)(2,1)S(1)} collective-permute-done((bf16[1,1,2,128,1024]{4,3,2,1,0:T(8,128)(2,1)S(1)}, bf16[1,1,2,128,1024]{4,3,2,1,0:T(8,128)(2,1)S(1)}, u32[]{:S(2)}, u32[]{:S(2)}) %collective-permute-start.6) | collective-permute-done | bytes 524320 | tf_op jit(solution)/shard_map/ppermute | solution.py:16
  56.5 10.6 collective-permute-done.2
  70.2 3.4 pad_maximum_fusion.2
  76.3 3.3 collective-permute-start.4
  90.0 111.9 %collective-permute-done.14 = s32[3,1,2,54]{3,2,1,0:T(2,128)S(1)} collective-permute-done((s32[3,1,2,54]{3,2,1,0:T(2,128)S(1)}, s32[3,1,2,54]{3,2,1,0:T(2,128)S(1)}, u32[]{:S(2)}, u32[]{:S(2)}) %collective-permute-start.14) | collective-permute-done | bytes 1328 | tf_op jit(solution)/shard_map/ppermute | solution.py:16
  201.9 4.1 collective-permute-done.15
  217.0 3.4 pad_maximum_fusion.3
  224.4 3.7 collective-permute-start.11
  228.1 8.6 pad_maximum_fusion
  236.8 8.6 fusion.110
  246.2 289.6 %while.106 = (s32[]{:T(128)}, bf16[2,128,512]{1,2,0:T(8,128)(2,1)}, f32[2,128,512]{1,2,0:T(8,128)}, f32[2,2,8,128]{3,2,1,0:T(8,128)S(1)}, f32[2,8]{1,0:T(2,128)S...) while((s32[]{:T(128)}, bf16[2,128,512]{1,2,0:T(8,128)(2,1)}, ...), condition=%wide.region_9.10_spmd.clone, body=%wide.region_3.9_spmd.clone.sunk | while | flops 238441568 | bytes 40497868 | solution.py:141
  247.5 5.0 gather_fusion.4
  252.4 4.9 gather_fusion.5
  257.4 132.1 %while.109 = (s32[]{:T(128)}, bf16[8,128,64]{1,2,0:T(8,128)(2,1)S(1)}, f32[8,128,64]{1,2,0:T(8,128)S(1)}, f32[8,128]{1,0:T(8,128)S(1)}, f32[8,128]{1,0:T(8,128)S...) while((s32[]{:T(128)}, ...), condition=%wide.region_8.8_spmd.clone, body=%wide.region_4.7_spmd.clone.sunk | while | flops 238436096 | bytes 25008588 | solution.py:131
  392.3 5.0 gather_fusion.4
  397.2 4.9 gather_fusion.5
  402.3 132.1 %while.109 = (s32[]{:T(128)}, bf16[8,128,64]{1,2,0:T(8,128)(2,1)S(1)}, f32[8,128,64]{1,2,0:T(8,128)S(1)}, f32[8,128]{1,0:T(8,128)S(1)}, f32[8,128]{1,0:T(8,128)S...) while((s32[]{:T(128)}, ...), condition=%wide.region_8.8_spmd.clone, body=%wide.region_4.7_spmd.clone.sunk | while | flops 238436096 | bytes 25008588 | solution.py:131
  538.6 7.7 pad_maximum_fusion.1
  546.3 8.5 fusion.109
  564.7 5.1 collective-permute-start.23
  573.1 263.4 %while.108 = (s32[]{:T(128)}, f32[2,128,512]{1,2,0:T(8,128)}, bf16[2,128,512]{1,2,0:T(8,128)(2,1)}, s32[2]{0:T(128)S(1)}, bf16[36,128,512]{2,1,0:T(8,128)(2,1)},...) while((s32[]{:T(128)}, f32[2,128,512]{1,2,0:T(8,128)}, ...), condition=%wide.region_15.16_spmd.clone, body=%wide.region_11.15_spmd.clone.sunk | while | flops 230034704 | bytes 25472284 | solution.py:199
  577.5 5.0 gather_fusion
  582.5 4.9 gather_fusion.2
  588.1 113.4 %while.110 = (s32[]{:T(128)}, f32[8,128,64]{1,2,0:T(8,128)}, bf16[8,128,64]{1,2,0:T(8,128)(2,1)}, s32[8]{0:T(128)S(1)}, bf16[3456,512]{1,0:T(8,128)(2,1)}, /*ind...) while((s32[]{:T(128)}, f32[8,128,64]{1,2,0:T(8,128)}, ...), condition=%wide.region_14.14_spmd.clone, body=%wide.region_13.13_spmd.clone.sunk | while | flops 230031360 | bytes 9096589 | solution.py:194
  592.7 3.3 fusion.158
  596.0 3.6 fusion.159
  606.9 3.3 fusion.158
  610.2 3.6 fusion.159
  621.1 3.3 fusion.158
  624.4 3.6 fusion.159
  635.3 3.3 fusion.158
  638.6 3.6 fusion.159
  649.5 3.3 fusion.158
  652.8 3.6 fusion.159
  663.6 3.3 fusion.158
  667.0 3.6 fusion.159
  677.8 3.3 fusion.158
  681.1 3.6 fusion.159
  692.0 3.3 fusion.158
  695.3 3.6 fusion.159
  709.2 5.0 gather_fusion
  714.2 4.9 gather_fusion.2
  719.8 113.4 %while.110 = (s32[]{:T(128)}, f32[8,128,64]{1,2,0:T(8,128)}, bf16[8,128,64]{1,2,0:T(8,128)(2,1)}, s32[8]{0:T(128)S(1)}, bf16[3456,512]{1,0:T(8,128)(2,1)}, /*ind...) while((s32[]{:T(128)}, f32[8,128,64]{1,2,0:T(8,128)}, ...), condition=%wide.region_14.14_spmd.clone, body=%wide.region_13.13_spmd.clone.sunk | while | flops 230031360 | bytes 9096589 | solution.py:194
  724.4 3.3 fusion.158
  727.7 3.6 fusion.159
  738.6 3.3 fusion.158
  741.9 3.6 fusion.159
  752.8 3.3 fusion.158
  756.1 3.6 fusion.159
  767.0 3.3 fusion.158
  770.3 3.6 fusion.159
  781.1 3.3 fusion.158
  784.5 3.6 fusion.159
  795.3 3.3 fusion.158
  798.6 3.6 fusion.159
  809.5 3.3 fusion.158
  812.8 3.6 fusion.159
  823.7 3.3 fusion.158
  827.0 3.6 fusion.159
  845.3 112.6 %all-reduce.7.cloned.1.call-done = (f32[512,512]{1,0:T(8,128)}, f32[512,512]{1,0:T(8,128)}, f32[512,512]{1,0:T(8,128)}, f32[512,512]{1,0:T(8,128)}) async-done(((f32[512,512]{1,0:T(8,128)}, f32[512,512]{1,0:T(8,128)}, f32[512,512]{1,0:T(8,128)}, f32[512,512]{1,0:T(8,128)}), (f32[512,512]{1,0:T(8,128)}, f32[512,512]{1,0:T(8,128)}, f32[512,512]{1,0:T(8,128)}, ...) | async-done | bytes 4194320 | tf_op jit(solution)/shard_map/psum | solution.py:218
  961.2 68.2 %all-reduce = (f32[512]{0:T(512)S(1)}, f32[8]{0:T(128)S(1)}) all-reduce(f32[512]{0:T(512)S(1)} %get-tuple-element.752, f32[8]{0:T(128)S(1)} %reduce_sum.117), channel_id=1, replica_groups=mesh['gx'=4,'gy'=4,'ta'=8] {'gy','ta'}, use_global_device_ids=true, to_apply=%region_19.20 | all-reduce | flops 520 | bytes 4160 | tf_op jit(solution)/shard_map/psum | solution.py:218
  1029.3 9.9 all-reduce.2
  1040.3 13.3 %all-reduce.9.cloned.1.call-done = (f32[512,512]{1,0:T(8,128)}, f32[512,512]{1,0:T(8,128)}, f32[512,512]{1,0:T(8,128)}, f32[512,512]{1,0:T(8,128)}) async-done(((f32[512,512]{1,0:T(8,128)}, f32[512,512]{1,0:T(8,128)}, f32[512,512]{1,0:T(8,128)}, f32[512,512]{1,0:T(8,128)}), (f32[512,512]{1,0:T(8,128)}, f32[512,512]{1,0:T(8,128)}, f32[512,512]{1,0:T(8,128)}, ...) | async-done | bytes 4194320 | tf_op jit(solution)/shard_map/psum | solution.py:217
  (551 shorter events, 390.5 us)
Async XLA Ops:
  7.2 4.9 copy-start
  7.2 4.9 copy-start.3
  7.2 4.9 copy-start.32
  7.2 950.7 %all-reduce.7.cloned.1.call-start = ((), (), s32[]{:S(2)}) async-start(), calls=%async_computation | async-start | bytes 8388608 | tf_op jit(solution)/shard_map/psum | solution.py:218
  8.4 8.5 copy-start.38
  9.9 7.0 copy-start.26
  12.1 216.0 %copy-start.5 = (bf16[2,128,512]{2,1,0:T(8,128)(2,1)}, bf16[2,128,512]{2,1,0:T(8,128)(2,1)S(1)}, u32[]{:S(2)}) copy-start(bf16[2,128,512]{2,1,0:T(8,128)(2,1)S(1)} %get-tuple-element.1510) | copy-start | bytes 786436
  12.4 215.7 %copy-start.7 = (bf16[2,128,512]{2,1,0:T(8,128)(2,1)}, bf16[2,128,512]{2,1,0:T(8,128)(2,1)S(1)}, u32[]{:S(2)}) copy-start(bf16[2,128,512]{2,1,0:T(8,128)(2,1)S(1)} %convolution_convert_fusion.1) | copy-start | bytes 786436
  13.3 15.3 %collective-permute-start = (bf16[1,1,2,128,1024]{4,3,2,1,0:T(8,128)(2,1)}, bf16[1,1,2,128,1024]{4,3,2,1,0:T(8,128)(2,1)S(1)}, u32[]{:S(2)}, u32[]{:S(2)}) collective-permute-start(bf16[1,1,2,128,1024]{4,3,2,1,0:T(8,128)(2,1)} %pad_maximum_fusion.6), channel_id=1, source_target_pairs={{0,32},{32,64},{64,96},{96,0},{1,33},{33,65},{65,97},{97,1},{2,34}... | collective-permute-start | bytes 1572872 | tf_op jit(solution)/shard_map/ppermute | solution.py:16
  15.5 13.1 %collective-permute-start.1 = (bf16[1,1,2,128,1024]{4,3,2,1,0:T(8,128)(2,1)}, bf16[1,1,2,128,1024]{4,3,2,1,0:T(8,128)(2,1)S(1)}, u32[]{:S(2)}, u32[]{:S(2)}) collective-permute-start(bf16[1,1,2,128,1024]{4,3,2,1,0:T(8,128)(2,1)} %pad_maximum_fusion.6), channel_id=1, source_target_pairs={{32,0},{64,32},{96,64},{0,96},{33,1},{65,33},{97,65},{1,97},{34,2}... | collective-permute-start | bytes 1572872 | tf_op jit(solution)/shard_map/ppermute | solution.py:19
  17.5 16.3 %copy-start.17 = (f32[2,128,512]{1,2,0:T(8,128)}, f32[2,128,512]{1,2,0:T(8,128)S(1)}, u32[]{:S(2)}) copy-start(f32[2,128,512]{1,2,0:T(8,128)S(1)} %copy.28) | copy-start | bytes 1572868
  28.6 10.6 copy-start.11
  29.9 37.1 %collective-permute-start.2 = (bf16[3,1,2,128,1024]{4,3,2,1,0:T(8,128)(2,1)}, bf16[3,1,2,128,1024]{4,3,2,1,0:T(8,128)(2,1)}, u32[]{:S(2)}, u32[]{:S(2)}) collective-permute-start(bf16[3,1,2,128,1024]{4,3,2,1,0:T(8,128)(2,1)} %pad_maximum_fusion.4), channel_id=1, source_target_pairs={{0,8},{8,16},{16,24},{24,0},{1,9},{9,17},{17,25},{25,1},{2,10},{10... | collective-permute-start | bytes 4718600 | tf_op jit(solution)/shard_map/ppermute | solution.py:16
  32.9 37.4 %collective-permute-start.3 = (bf16[3,1,2,128,1024]{4,3,2,1,0:T(8,128)(2,1)}, bf16[3,1,2,128,1024]{4,3,2,1,0:T(8,128)(2,1)}, u32[]{:S(2)}, u32[]{:S(2)}) collective-permute-start(bf16[3,1,2,128,1024]{4,3,2,1,0:T(8,128)(2,1)} %pad_maximum_fusion.4), channel_id=1, source_target_pairs={{8,0},{16,8},{24,16},{0,24},{9,1},{17,9},{25,17},{1,25},{10,2},{18... | collective-permute-start | bytes 4718600 | tf_op jit(solution)/shard_map/ppermute | solution.py:19
  39.2 31.0 %copy-start.12 = (bf16[1,1,2,128,1024]{4,3,2,1,0:T(8,128)(2,1)S(1)}, bf16[1,1,2,128,1024]{4,3,2,1,0:T(8,128)(2,1)}, u32[]{:S(2)}) copy-start(bf16[1,1,2,128,1024]{4,3,2,1,0:T(8,128)(2,1)} %copy-done.11) | copy-start | bytes 1572868
  39.3 14.6 %collective-permute-start.6 = (bf16[1,1,2,128,1024]{4,3,2,1,0:T(8,128)(2,1)S(1)}, bf16[1,1,2,128,1024]{4,3,2,1,0:T(8,128)(2,1)S(1)}, u32[]{:S(2)}, u32[]{:S(2)}) collective-permute-start(bf16[1,1,2,128,1024]{4,3,2,1,0:T(8,128)(2,1)S(1)} %pad_maximum_fusion.7), channel_id=1, source_target_pairs={{0,32},{32,64},{64,96},{96,0},{1,33},{33,65},{65,97},{97,1},{2,34}... | collective-permute-start | bytes 1572872 | tf_op jit(solution)/shard_map/ppermute | solution.py:16
  40.7 13.2 %collective-permute-start.7 = (bf16[1,1,2,128,1024]{4,3,2,1,0:T(8,128)(2,1)S(1)}, bf16[1,1,2,128,1024]{4,3,2,1,0:T(8,128)(2,1)S(1)}, u32[]{:S(2)}, u32[]{:S(2)}) collective-permute-start(bf16[1,1,2,128,1024]{4,3,2,1,0:T(8,128)(2,1)S(1)} %pad_maximum_fusion.7), channel_id=1, source_target_pairs={{32,0},{64,32},{96,64},{0,96},{33,1},{65,33},{97,65},{1,97},{34,2}... | collective-permute-start | bytes 1572872 | tf_op jit(solution)/shard_map/ppermute | solution.py:19
  53.9 163.1 %copy-start.9 = (bf16[1,1,2,128,1024]{4,3,2,1,0:T(8,128)(2,1)}, bf16[1,1,2,128,1024]{4,3,2,1,0:T(8,128)(2,1)S(1)}, u32[]{:S(2)}) copy-start(bf16[1,1,2,128,1024]{4,3,2,1,0:T(8,128)(2,1)S(1)} %collective-permute-done.6) | copy-start | bytes 1572868
  53.9 163.1 %copy-start.10 = (bf16[1,1,2,128,1024]{4,3,2,1,0:T(8,128)(2,1)}, bf16[1,1,2,128,1024]{4,3,2,1,0:T(8,128)(2,1)S(1)}, u32[]{:S(2)}) copy-start(bf16[1,1,2,128,1024]{4,3,2,1,0:T(8,128)(2,1)S(1)} %collective-permute-done.7) | copy-start | bytes 1572868
  55.4 161.5 %collective-permute-start.8 = (bf16[3,1,2,128,1024]{4,3,2,1,0:T(8,128)(2,1)}, bf16[3,1,2,128,1024]{4,3,2,1,0:T(8,128)(2,1)}, u32[]{:S(2)}, u32[]{:S(2)}) collective-permute-start(bf16[3,1,2,128,1024]{4,3,2,1,0:T(8,128)(2,1)} %pad_maximum_fusion.5), channel_id=1, source_target_pairs={{0,8},{8,16},{16,24},{24,0},{1,9},{9,17},{17,25},{25,1},{2,10},{10... | collective-permute-start | bytes 4718600 | tf_op jit(solution)/shard_map/ppermute | solution.py:16
  56.5 160.5 %collective-permute-start.9 = (bf16[3,1,2,128,1024]{4,3,2,1,0:T(8,128)(2,1)}, bf16[3,1,2,128,1024]{4,3,2,1,0:T(8,128)(2,1)}, u32[]{:S(2)}, u32[]{:S(2)}) collective-permute-start(bf16[3,1,2,128,1024]{4,3,2,1,0:T(8,128)(2,1)} %pad_maximum_fusion.5), channel_id=1, source_target_pairs={{8,0},{16,8},{24,16},{0,24},{9,1},{17,9},{25,17},{1,25},{10,2},{18... | collective-permute-start | bytes 4718600 | tf_op jit(solution)/shard_map/ppermute | solution.py:19
  73.7 8.2 copy-start.40
  73.7 8.2 copy-start.41
  76.3 151.8 %collective-permute-start.4 = (bf16[3,3,1,128,1024]{4,3,2,1,0:T(8,128)(2,1)}, bf16[3,3,1,128,1024]{4,3,2,1,0:T(8,128)(2,1)}, u32[]{:S(2)}, u32[]{:S(2)}) collective-permute-start(bf16[3,3,1,128,1024]{4,3,2,1,0:T(8,128)(2,1)} %get-tuple-element.896), channel_id=1, source_target_pairs={{0,1},{1,2},{2,3},{3,4},{4,5},{5,6},{6,7},{7,0},{8,9},{9,10},{10,1... | collective-permute-start | bytes 7077896 | tf_op jit(solution)/shard_map/ppermute | solution.py:16
  79.6 148.5 %collective-permute-start.5 = (bf16[3,3,1,128,1024]{4,3,2,1,0:T(8,128)(2,1)}, bf16[3,3,1,128,1024]{4,3,2,1,0:T(8,128)(2,1)}, u32[]{:S(2)}, u32[]{:S(2)}) collective-permute-start(bf16[3,3,1,128,1024]{4,3,2,1,0:T(8,128)(2,1)} %get-tuple-element.897), channel_id=1, source_target_pairs={{1,0},{2,1},{3,2},{4,3},{5,4},{6,5},{7,6},{0,7},{9,8},{10,9},{11,1... | collective-permute-start | bytes 7077896 | tf_op jit(solution)/shard_map/ppermute | solution.py:19
  81.9 4.0 collective-permute-start.12
  85.9 2.8 collective-permute-start.13
  88.8 113.1 %collective-permute-start.14 = (s32[3,1,2,54]{3,2,1,0:T(2,128)S(1)}, s32[3,1,2,54]{3,2,1,0:T(2,128)S(1)}, u32[]{:S(2)}, u32[]{:S(2)}) collective-permute-start(s32[3,1,2,54]{3,2,1,0:T(2,128)S(1)} %pad_add_fusion.2), channel_id=1, source_target_pairs={{0,8},{8,16},{16,24},{24,0},{1,9},{9,17},{17,25},{25,1},{2,10},{10... | collective-permute-start | bytes 3896 | tf_op jit(solution)/shard_map/ppermute | solution.py:16
  201.9 4.1 collective-permute-start.15
  206.1 6.1 collective-permute-start.16
  212.3 4.0 collective-permute-start.17
  220.4 7.7 copy-start.13
  223.0 315.6 %collective-permute-start.10 = (bf16[3,3,1,128,1024]{4,3,2,1,0:T(8,128)(2,1)}, bf16[3,3,1,128,1024]{4,3,2,1,0:T(8,128)(2,1)}, u32[]{:S(2)}, u32[]{:S(2)}) collective-permute-start(bf16[3,3,1,128,1024]{4,3,2,1,0:T(8,128)(2,1)} %get-tuple-element.894), channel_id=1, source_target_pairs={{0,1},{1,2},{2,3},{3,4},{4,5},{5,6},{6,7},{7,0},{8,9},{9,10},{10,1... | collective-permute-start | bytes 7077896 | tf_op jit(solution)/shard_map/ppermute | solution.py:16
  224.4 314.2 %collective-permute-start.11 = (bf16[3,3,1,128,1024]{4,3,2,1,0:T(8,128)(2,1)}, bf16[3,3,1,128,1024]{4,3,2,1,0:T(8,128)(2,1)}, u32[]{:S(2)}, u32[]{:S(2)}) collective-permute-start(bf16[3,3,1,128,1024]{4,3,2,1,0:T(8,128)(2,1)} %get-tuple-element.895), channel_id=1, source_target_pairs={{1,0},{2,1},{3,2},{4,3},{5,4},{6,5},{7,6},{0,7},{9,8},{10,9},{11,1... | collective-permute-start | bytes 7077896 | tf_op jit(solution)/shard_map/ppermute | solution.py:19
  236.8 9.4 copy-start.43
  535.8 22.1 %collective-permute-start.18 = (f32[1,1,2,2,8,128]{5,4,3,2,1,0:T(8,128)S(1)}, f32[1,1,2,2,8,128]{5,4,3,2,1,0:T(8,128)S(1)}, u32[]{:S(2)}, u32[]{:S(2)}) collective-permute-start(f32[1,1,2,2,8,128]{5,4,3,2,1,0:T(8,128)S(1)} %bitcast.281), channel_id=1, source_target_pairs={{0,32},{32,64},{64,96},{96,0},{1,33},{33,65},{65,97},{97,1},{2,34}... | collective-permute-start | bytes 49160 | tf_op jit(solution)/shard_map/ppermute | solution.py:16
  537.2 20.7 %collective-permute-start.19 = (f32[1,1,2,2,8,128]{5,4,3,2,1,0:T(8,128)S(1)}, f32[1,1,2,2,8,128]{5,4,3,2,1,0:T(8,128)S(1)}, u32[]{:S(2)}, u32[]{:S(2)}) collective-permute-start(f32[1,1,2,2,8,128]{5,4,3,2,1,0:T(8,128)S(1)} %bitcast.282), channel_id=1, source_target_pairs={{32,0},{64,32},{96,64},{0,96},{33,1},{65,33},{97,65},{1,97},{34,2}... | collective-permute-start | bytes 49160 | tf_op jit(solution)/shard_map/ppermute | solution.py:19
  546.3 8.6 copy-start.20
  546.3 9.6 copy-start.18
  546.3 9.6 copy-start.37
  554.8 2.9 copy-start.30
  555.9 13.8 %copy-start.4 = (bf16[1,1,2,128,512]{4,3,2,1,0:T(8,128)(2,1)S(1)}, bf16[1,1,2,128,512]{4,3,2,1,0:T(8,128)(2,1)}, u32[]{:S(2)}) copy-start(bf16[1,1,2,128,512]{4,3,2,1,0:T(8,128)(2,1)} %param.18) | copy-start | bytes 786436
  555.9 13.8 %copy-start.33 = (f32[512]{0:T(512)S(1)}, f32[512]{0:T(512)}, u32[]{:S(2)}) copy-start(f32[512]{0:T(512)} %param.19) | copy-start | bytes 6148
  556.0 13.8 %copy-start.39 = (f32[2,128]{1,0:T(2,128)S(1)}, f32[2,128]{1,0:T(2,128)}, u32[]{:S(2)}) copy-start(f32[2,128]{1,0:T(2,128)} %copy-done.38) | copy-start | bytes 3076
  556.2 16.8 %copy-start.2 = (s32[36,54]{1,0:T(8,128)S(1)}, s32[36,54]{1,0:T(8,128)}, u32[]{:S(2)}) copy-start(s32[36,54]{1,0:T(8,128)} %reshape.687) | copy-start | bytes 23332
  556.2 16.8 %copy-start.6 = (bf16[2,128,512]{2,1,0:T(8,128)(2,1)S(1)}, bf16[2,128,512]{2,1,0:T(8,128)(2,1)}, u32[]{:S(2)}) copy-start(bf16[2,128,512]{2,1,0:T(8,128)(2,1)} %copy-done.5) | copy-start | bytes 786436
  556.3 16.8 %copy-start.8 = (bf16[2,128,512]{2,1,0:T(8,128)(2,1)S(1)}, bf16[2,128,512]{2,1,0:T(8,128)(2,1)}, u32[]{:S(2)}) copy-start(bf16[2,128,512]{2,1,0:T(8,128)(2,1)} %copy-done.7) | copy-start | bytes 786436
  556.3 16.8 %copy-start.42 = (s32[9]{0:T(128)S(1)}, s32[9]{0:T(128)}, u32[]{:S(2)}) copy-start(s32[9]{0:T(128)} %iota_multiply_fusion) | copy-start | bytes 112
  557.7 15.4 %copy-start.21 = (bf16[2,128,512]{2,1,0:T(8,128)(2,1)}, bf16[2,128,512]{2,1,0:T(8,128)(2,1)S(1)}, u32[]{:S(2)}) copy-start(bf16[2,128,512]{2,1,0:T(8,128)(2,1)S(1)} %multiply_convert_fusion.3) | copy-start | bytes 786436
  557.9 5.3 collective-permute-start.20
  561.0 3.6 collective-permute-start.21
  564.6 6.9 collective-permute-start.22
  564.7 6.8 collective-permute-start.23
  573.1 265.6 %copy-start.35 = (f32[2,128,8]{1,2,0:T(8,128)S(1)}, f32[2,128,8]{1,2,0:T(8,128)}, u32[]{:S(2)}) copy-start(f32[2,128,8]{1,2,0:T(8,128)} %copy-done.34) | copy-start | bytes 24580
  836.5 4.5 copy-start.15
  836.5 4.5 copy-start.27
  838.6 5.2 copy-start.23
  845.2 112.7 %copy-start.25 = (bf16[512,512]{1,0:T(8,128)(2,1)S(1)}, bf16[512,512]{1,0:T(8,128)(2,1)}, u32[]{:S(2)}) copy-start(bf16[512,512]{1,0:T(8,128)(2,1)} %param.23) | copy-start | bytes 1572868
  845.2 112.7 %copy-start.31 = (bf16[2,128,512]{1,2,0:T(8,128)(2,1)S(1)}, bf16[2,128,512]{1,2,0:T(8,128)(2,1)}, u32[]{:S(2)}) copy-start(bf16[2,128,512]{1,2,0:T(8,128)(2,1)} %get-tuple-element.1644) | copy-start | bytes 786436
  845.3 113.7 %copy-start.22 = (bf16[2,128,512]{2,1,0:T(8,128)(2,1)S(1)}, bf16[2,128,512]{2,1,0:T(8,128)(2,1)}, u32[]{:S(2)}) copy-start(bf16[2,128,512]{2,1,0:T(8,128)(2,1)} %copy-done.21) | copy-start | bytes 786436
  845.3 115.1 %copy-start.24 = (bf16[512,512]{1,0:T(8,128)(2,1)S(1)}, bf16[512,512]{1,0:T(8,128)(2,1)}, u32[]{:S(2)}) copy-start(bf16[512,512]{1,0:T(8,128)(2,1)} %param.21) | copy-start | bytes 1572868
  845.3 208.3 %all-reduce.9.cloned.1.call-start = ((), (), s32[]{:S(2)}) async-start(), calls=%async_computation.1 | async-start | bytes 8388608 | tf_op jit(solution)/shard_map/psum | solution.py:217
  1053.6 4.7 copy-start.29
  1053.6 5.7 copy-start.28
  (21 other events, 26.8 us)
Sparse Core Ops, SparseCore 0:
  845.4 112.4 all-reduce.6
  960.4 93.1 all-reduce.8
